TPU v7x, 256 devices: a whole 4x4x8 slice. The times are simulated.
256 devices in a mesh: env: 16 (over x, y_lo, core), pts: 16 (over y_hi, z).
Axes of the slice: x: 4, y: 4 (y_hi: 2, y_lo: 2; y = y_hi * 2 + y_lo), z: 8, core: 2. Of those that a mesh axis runs over, the one named last changes fastest.
Arguments:
- descriptors: float32 [1024, 16384], P('pts', 'env'), may hold values from -6 to 6
- env_weight: float32 [16384], P('env'), may hold values from 0.25 to 4
- points: float32 [2560, 1024], P('pts', 'env'), may hold values from -6 to 6
Outputs:
- panel_factor: float32 [2560, 512], P('env', 'pts')
- trailing: float32 [2048, 2048], P('env', 'pts')
All inputs are finite; a program needn't handle non-finite values.
Results may differ from a plain program's by a relative error of at most 0.0003.
Values sent between devices are 32-bit elements; how exact they have to be, the bound alone decides.
A program may use at most 64 MiB of HBM per device.

v0:
```python
import jax
import jax.numpy as jnp
from jax import lax
from jax.sharding import Mesh
from jax.sharding import PartitionSpec as P

PANEL = 512
PTS = ("pts_0", "pts_1")
ENV_PTS = ("env", "pts_0", "pts_1")


def joined_along(blocks, dim):
    lengths = list(blocks.shape[1:])
    lengths[dim] *= blocks.shape[0]
    return jnp.moveaxis(blocks, 0, dim).reshape(lengths)


def gather_in_order(shard, axes, order):
    blocks = shard[None]
    for k in order:
        blocks = lax.all_gather(blocks, axes[k], axis=0, tiled=True)
    held = [lax.axis_size(axes[k]) for k in reversed(order)]
    blocks = blocks.reshape(*held, *shard.shape)
    turned = sorted(range(len(order)), key=lambda place: order[len(order) - 1 - place])
    return blocks.transpose(*turned, *range(len(order), blocks.ndim)).reshape(-1, *shard.shape)


def gathered_by_axis(shard, axes, order, dim):
    return joined_along(gather_in_order(shard, axes, order), dim)


def cut_along(shard, dim, count):
    before, after = (shard.shape[:dim], shard.shape[dim + 1 :])
    return jnp.moveaxis(shard.reshape(*before, count, -1, *after), dim, 0)


def summed_on_arrival(shard, axis, dim):
    count = lax.axis_size(axis)
    blocks = lax.all_to_all(cut_along(shard, dim, count), axis, 0, 0, tiled=True)
    return jnp.sum(blocks, axis=0)


def cubed_kernel(features, targets):
    dots = lax.dot_general(
        features,
        targets,
        (((0,), (1,)), ((), ())),
        precision=lax.Precision.HIGH,
        preferred_element_type=jnp.float32,
    )
    scaled = dots / jnp.sqrt(jnp.float32(features.shape[0]))
    return 0.25 * scaled * scaled * scaled


def local_points(count, device, devices, block_size):
    positions = jnp.arange(count, dtype=jnp.int32)
    return block_size * (devices * (positions // block_size) + device) + positions % block_size


def local(descriptors, env_weight, points):
    env_count = lax.axis_size("env")
    pts_count = lax.axis_size(PTS)
    env_rank = lax.axis_index("env")
    pts_rank = lax.axis_index(PTS)
    features = gathered_by_axis(descriptors, PTS, (0, 1), 0)
    own_points = lax.all_gather(points, "env", axis=1, tiled=True)
    cols_dev = own_points.shape[0]
    total_points = cols_dev * pts_count
    rows_dev = total_points // env_count
    row_block = PANEL // env_count
    col_block = PANEL // pts_count
    cycles = total_points // PANEL
    own_tile = cubed_kernel(features, own_points)
    weighted = own_tile * env_weight[:, None]
    partial_gram = lax.dot_general(
        lax.all_gather(own_tile, PTS, axis=1, tiled=True),
        weighted,
        (((0,), (0,)), ((), ())),
        precision=lax.Precision.HIGH,
        preferred_element_type=jnp.float32,
    )
    partial_gram = partial_gram / jnp.float32(descriptors.shape[1] * env_count)
    natural = (
        partial_gram.reshape(pts_count, cycles, col_block, cols_dev)
        .transpose(1, 0, 2, 3)
        .reshape(total_points, cols_dev)
    )
    by_rows = (
        natural.reshape(cycles, env_count, row_block, cols_dev)
        .transpose(1, 0, 2, 3)
        .reshape(total_points, cols_dev)
    )
    gram_block = summed_on_arrival(by_rows, "env", 0)
    row_ids = local_points(rows_dev, env_rank, env_count, row_block)
    col_ids = local_points(cols_dev, pts_rank, pts_count, col_block)
    gram_block = gram_block + (row_ids[:, None] == col_ids[None, :]).astype(jnp.float32)
    panel_rows = lax.all_gather(gram_block[:, :col_block], PTS, axis=1, tiled=True)
    leading = lax.all_gather(panel_rows[:row_block], "env", axis=0, tiled=True)
    low_factor = jnp.linalg.cholesky(leading)
    row_factor = jax.scipy.linalg.solve_triangular(low_factor, panel_rows.T, lower=True).T
    panel_out = lax.dynamic_slice_in_dim(row_factor, pts_rank * col_block, col_block, 1)
    top_rows = lax.all_gather(gram_block[:row_block, :], "env", axis=0, tiled=True)
    side_factor = jax.scipy.linalg.solve_triangular(low_factor, top_rows, lower=True).T[col_block:]
    update = lax.dot_general(
        row_factor[row_block:],
        side_factor,
        (((1,), (1,)), ((), ())),
        precision=lax.Precision.HIGHEST,
        preferred_element_type=jnp.float32,
    )
    trailing = gram_block[row_block:, col_block:] - update
    return (panel_out, trailing)


def solution(mesh):
    finer = Mesh(mesh.devices.reshape(mesh.shape["env"], 2, 8), ("env", "pts_0", "pts_1"))
    placed = (P(PTS, "env"), P("env"), P(PTS, "env"))
    return jax.shard_map(
        local,
        mesh=finer,
        in_specs=placed,
        out_specs=(P("env", PTS), P("env", PTS)),
        check_vma=False,
    )
```

profile of v0, /device:TPU:1, one launch (start us, length us, event | category | flops | bytes accessed | tf_op | source)
XLA Modules:
  0.0 520.1 jit_solution(16651984961840194268)
XLA Ops:
  7.2 12.0 %all-gather = f32[128,1024]{1,0:T(8,128)} all-gather(f32[64,1024]{1,0:T(8,128)} %param.5), channel_id=2, replica_groups=mesh['env'=16,'pts_0'=2,'pts_1'=8] {'pts_0'}, dimensions={0}, use_global_device_ids=true | all-gather | bytes 786432 | tf_op jit(solution)/shard_map/all_gather | solution.py:21
  19.3 23.6 %all_gather.23 = f32[160,1024]{0,1:T(8,128)S(1)} all-gather(f32[160,64]{0,1:T(8,128)} %param.7), channel_id=1, replica_groups=mesh['env'=16,'pts_0'=2,'pts_1'=8] {'env'}, dimensions={1}, use_global_device_ids=true | all-gather | bytes 696320 | tf_op jit(solution)/shard_map/all_gather | solution.py:66
  42.9 33.4 %all-gather.5.cloned.1.call-done = f32[16,64,1024]{2,1,0:T(8,128)} async-done(((f32[2,64,1024]{2,1,0:T(8,128)}), f32[16,64,1024]{2,1,0:T(8,128)}) %all-gather.5.cloned.1.call-update) | async-done | bytes 4194320 | tf_op jit(solution)/shard_map/all_gather | solution.py:21
  76.3 2.5 copy.28
  78.8 2.3 multiply_multiply_fusion
  81.1 154.6 %all-gather.7.cloned.1.call-done = f32[1024,2560]{0,1:T(8,128)} async-done(((f32[1024,160]{0,1:T(8,128)}), f32[1024,2560]{0,1:T(8,128)}) %all-gather.7.cloned.1.call-update) | async-done | bytes 10485776 | tf_op jit(solution)/shard_map/all_gather | solution.py:76
  235.7 10.6 %convolution_multiply_fusion = f32[2560,160]{0,1:T(8,128)} fusion(f32[1024,2560]{0,1:T(8,128)} %all-gather.7.cloned.1.call-done, f32[1024]{0:T(1024)S(1)} %copy-done.2, f32[1024,160]{0,1:T(8,128)S(1)} %get-tuple-element.55), kind=kOutput, calls=%fused_computation.2 | convolution fusion | flops 2517811200 | bytes 12783616 | tf_op jit(solution)/shard_map/dot_general | solution.py:75
  246.3 2.6 reshape_reshape_reshape.3
  248.9 3.0 copy.29
  251.9 5.7 %all-to-all-start = ((f32[16,160,160]{1,2,0:T(8,128)}), f32[16,160,160]{1,2,0:T(8,128)S(1)}, u32[]{:S(2)}, u32[]{:S(2)}) async-start(f32[16,160,160]{1,2,0:T(8,128)} %copy.29), calls=%async_computation | async-start | bytes 5242880 | tf_op jit(solution)/shard_map/all_to_all | solution.py:39
  257.6 33.3 %all-to-all-done = f32[16,160,160]{1,2,0:T(8,128)S(1)} async-done(((f32[16,160,160]{1,2,0:T(8,128)}), f32[16,160,160]{1,2,0:T(8,128)S(1)}, u32[]{:S(2)}, u32[]{:S(2)}) %all-to-all-start) | async-done | bytes 1638432 | tf_op jit(solution)/shard_map/all_to_all | solution.py:39
  291.4 34.4 %all_gather.25 = f32[160,512]{0,1:T(8,128)S(1)} all-gather(f32[160,32]{0,1:T(8,128)S(1)} %copy.31), channel_id=1, replica_groups=mesh['env'=16,'pts_0'=2,'pts_1'=8] {'pts_0','pts_1'}, dimensions={1}, use_global_device_ids=true | all-gather | bytes 348160 | tf_op jit(solution)/shard_map/all_gather | solution.py:97
  325.8 0.7 copy.32
  326.6 0.6 iota_multiply_fusion
  327.3 28.4 %all_gather.27 = f32[512,160]{1,0:T(8,128)S(1)} all-gather(f32[32,160]{1,0:T(8,128)S(1)} %slice.144), channel_id=1, replica_groups=mesh['env'=16,'pts_0'=2,'pts_1'=8] {'env'}, dimensions={0}, use_global_device_ids=true | all-gather | bytes 348160 | tf_op jit(solution)/shard_map/all_gather | solution.py:102
  355.8 0.8 copy-done
  356.7 0.7 copy.40
  357.5 0.7 copy.39
  358.2 6.9 %all-gather.9.cloned.1.call-done = f32[512,512]{1,0:T(8,128)} async-done(((f32[32,512]{1,0:T(8,128)}), f32[512,512]{1,0:T(8,128)}) %all-gather.9.cloned.1.call-update) | async-done | bytes 1048592 | tf_op jit(solution)/shard_map/all_gather | solution.py:98
  365.1 1.6 copy.33
  366.7 1.4 fusion
  368.2 11.7 %cholesky.104 = f32[128,128]{1,0:T(8,128)S(1)} custom-call(f32[128,128]{1,0:T(8,128)S(1)} %cholesky.266), custom_call_target="Cholesky" | custom-call | tf_op jit(solution)/shard_map/jit(cholesky)/cholesky | solution.py:99
  380.0 9.8 %custom-call.30 = f32[1,128,128]{1,2,0:T(8,128)S(1)} custom-call(f32[1,128,128]{2,1,0:T(8,128)S(1)} %get-tuple-element.53), custom_call_target="InvertDiagBlocksLowerTriangular" | custom-call | tf_op jit(solution)/shard_map/jit(cholesky)/cholesky | solution.py:99
  389.9 0.3 constant_dynamic-update-slice_fusion.3
  390.2 0.3 convolution_subtract_fusion
  390.5 11.7 %cholesky.217 = f32[128,128]{1,0:T(8,128)S(1)} custom-call(f32[128,128]{1,0:T(8,128)S(1)} %cholesky.270), custom_call_target="Cholesky" | custom-call | tf_op jit(solution)/shard_map/jit(cholesky)/cholesky | solution.py:99
  402.3 10.0 %custom-call.31 = f32[1,128,128]{1,2,0:T(8,128)S(1)} custom-call(f32[1,128,128]{2,1,0:T(8,128)S(1)} %get-tuple-element.50), custom_call_target="InvertDiagBlocksLowerTriangular" | custom-call | tf_op jit(solution)/shard_map/jit(cholesky)/cholesky | solution.py:99
  412.2 0.3 convolution_dynamic-update-slice_fusion
  412.5 0.4 convolution_subtract_fusion.1
  412.9 11.7 %cholesky.238 = f32[128,128]{1,0:T(8,128)S(1)} custom-call(f32[128,128]{1,0:T(8,128)S(1)} %cholesky.275), custom_call_target="Cholesky" | custom-call | tf_op jit(solution)/shard_map/jit(cholesky)/cholesky | solution.py:99
  424.7 9.8 %custom-call.32 = f32[1,128,128]{1,2,0:T(8,128)S(1)} custom-call(f32[1,128,128]{2,1,0:T(8,128)S(1)} %get-tuple-element.47), custom_call_target="InvertDiagBlocksLowerTriangular" | custom-call | tf_op jit(solution)/shard_map/jit(cholesky)/cholesky | solution.py:99
  434.7 0.4 convolution_subtract_fusion.9
  435.1 11.9 %cholesky.255 = f32[128,128]{1,0:T(8,128)S(1)} custom-call(f32[128,128]{1,0:T(8,128)S(1)} %convolution_subtract_fusion.9), custom_call_target="Cholesky" | custom-call | tf_op jit(solution)/shard_map/jit(cholesky)/cholesky | solution.py:99
  447.0 0.6 compare_reduce_fusion.3
  447.6 0.7 compare_reduce_fusion.2
  448.4 0.6 compare_reduce_fusion.1
  449.0 0.7 compare_reduce_fusion
  452.3 0.7 triangular_solve.123
  453.0 10.9 %while.4 = (s32[]{:T(128)}, f32[512,512]{1,0:T(8,128)S(1)}, s32[4,2]{0,1:T(2,128)S(1)}, f32[4,128,128]{2,1,0:T(8,128)}, s32[]{:T(128)}) while((s32[]{:T(128)}, f32[512,512]{1,0:T(8,128)S(1)}, s32[4,2]{0,1:T(2,128)S(1)}, f32[4,128,128]{2,1,0:T(8,128)}, s32[]{:T(128)}) %tuple.45), condition=%wide.while_cond, body=%wide.while_body.sunk | while | flops 2 | bytes 132205 | solution.py:100
  453.0 0.6 fusion.71
  453.6 2.0 bitcast_dynamic-update-slice_fusion.2
  455.8 0.6 fusion.71
  456.4 2.1 bitcast_dynamic-update-slice_fusion.2
  458.5 0.6 fusion.71
  459.1 2.0 bitcast_dynamic-update-slice_fusion.2
  461.2 0.6 fusion.71
  461.8 2.1 bitcast_dynamic-update-slice_fusion.2
  463.8 40.1 %custom-call.34 = f32[4,128,128]{1,2,0:T(8,128)S(1)} custom-call(f32[4,128,128]{2,1,0:T(8,128)} %get-tuple-element.17), custom_call_target="InvertDiagBlocksLowerTriangular" | custom-call | tf_op jit(solution)/shard_map/jit(_solve_triangular)/triangular_solve | solution.py:100
  504.0 1.3 fusion.27
  505.2 0.2 fusion.33
  505.5 0.3 convolution_subtract_fusion.3
  505.7 0.2 fusion.41
  506.0 0.3 convolution_subtract_fusion.7
  506.3 0.2 fusion.43
  506.5 0.4 convolution_subtract_fusion.6
  506.9 0.2 fusion.45
  507.3 0.7 copy.38
  508.0 1.2 convolution_subtract_fusion.2
  509.1 0.2 fusion.40
  509.4 1.2 convolution_subtract_fusion.5
  510.6 0.2 fusion.42
  510.8 0.4 convolution_subtract_fusion.4
  511.2 0.2 fusion.44
  511.4 1.9 convolution_subtract_fusion.8
  (40 shorter events, 2.0 us)
Async XLA Ops:
  7.2 69.1 %all-gather.5.cloned.1.call-start = ((), (), s32[]{:S(2)}) async-start(), calls=%async_computation.1 | async-start | bytes 4718592 | tf_op jit(solution)/shard_map/all_gather | solution.py:21
  19.2 216.5 %all-gather.7.cloned.1.call-start = ((), (), s32[]{:S(2)}) async-start(), calls=%async_computation.2 | async-start | bytes 11141120 | tf_op jit(solution)/shard_map/all_gather | solution.py:76
  78.8 156.9 %copy-start.2 = (f32[1024]{0:T(1024)S(1)}, f32[1024]{0:T(1024)}, u32[]{:S(2)}) copy-start(f32[1024]{0:T(1024)} %param.6) | copy-start | bytes 12292
  251.9 39.1 %all-to-all-start = ((f32[16,160,160]{1,2,0:T(8,128)}), f32[16,160,160]{1,2,0:T(8,128)S(1)}, u32[]{:S(2)}, u32[]{:S(2)}) async-start(f32[16,160,160]{1,2,0:T(8,128)} %copy.29), calls=%async_computation | async-start | bytes 5242880 | tf_op jit(solution)/shard_map/all_to_all | solution.py:39
  257.6 107.6 %all-gather.9.cloned.1.call-start = ((), (), s32[]{:S(2)}) async-start(), calls=%async_computation.3 | async-start | bytes 1114112 | tf_op jit(solution)/shard_map/all_gather | solution.py:98
  291.3 66.9 %copy-start.1 = (f32[160,160]{1,0:T(8,128)}, f32[160,160]{1,0:T(8,128)S(1)}, u32[]{:S(2)}) copy-start(f32[160,160]{1,0:T(8,128)S(1)} %convert_add_fusion) | copy-start | bytes 307204
  355.8 0.8 copy-start
Sparse Core Ops, SparseCore 0:
  19.3 56.9 all-gather.4
  81.2 154.4 all-gather.6
  326.7 38.3 all-gather.8
where the time goes:
time: 528 us; the launch traced here: 520 us
  waiting for transfers between devices  228 us (43%)
  other arithmetic  122 us (23%)
  blocking collectives  98.4 us (19%)
  local copies, waits for them, and re-layouts  25.6 us (5%)
  matrix products  23.1 us (4%)
  between operations  16.8 us (3%)
  starting transfers between devices  5.81 us (1%)
    all_gather x1, waiting for transfers between devices, local(): lax.all_gather(own_tile, PTS, axis=1, tiled=True)  155 us
    another operation x15, other arithmetic, local(): low_factor = jnp.linalg.cholesky(leading)  79.4 us
    another operation x4, other arithmetic, local(): jax.scipy.linalg.solve_triangular(low_factor, panel_rows.T, lower=True)  40.8 us
    all_gather x1, blocking collectives, local(): lax.all_gather(gram_block[:, :col_block], PTS, axis=1, tiled=True)  34.4 us
    all_gather x1, waiting for transfers between devices, gather_in_order(): blocks = lax.all_gather(blocks, axes[k], axis=0, tiled=True)  33.4 us
    all_to_all x1, waiting for transfers between devices, summed_on_arrival(): lax.all_to_all(cut_along(shard, dim, count), axis, 0, 0, tiled=True)  33.3 us
    all_gather x1, blocking collectives, local(): lax.all_gather(gram_block[:row_block, :], 'env', axis=0, tiled=True)  28.4 us
    all_gather x1, blocking collectives, local(): own_points = lax.all_gather(points, 'env', axis=1, tiled=True)  23.6 us
  transfers between devices with their start and end apart: 4, of which 4 were waited for; matrix products, arithmetic and copies ran while one was open for 0% of the time, Pallas kernels for 0%

commit v1 on v0

--- a/solution.py
+++ b/solution.py
@@ -7,6 +7,16 @@
 PANEL = 512
 PTS = ("pts_0", "pts_1")
 ENV_PTS = ("env", "pts_0", "pts_1")
+
+
+def enter_column(x_local):
+    block_last = jnp.concatenate(
+        lax.all_to_all(
+            jnp.stack(lax.axis_size(PTS) * [x_local]), axis_name=PTS, split_axis=0, concat_axis=0
+        ),
+        axis=1,
+    )
+    return block_last
 
 
 def joined_along(blocks, dim):
@@ -94,7 +104,7 @@
     row_ids = local_points(rows_dev, env_rank, env_count, row_block)
     col_ids = local_points(cols_dev, pts_rank, pts_count, col_block)
     gram_block = gram_block + (row_ids[:, None] == col_ids[None, :]).astype(jnp.float32)
-    panel_rows = lax.all_gather(gram_block[:, :col_block], PTS, axis=1, tiled=True)
+    panel_rows = enter_column(gram_block[:, :col_block])
     leading = lax.all_gather(panel_rows[:row_block], "env", axis=0, tiled=True)
     low_factor = jnp.linalg.cholesky(leading)
     row_factor = jax.scipy.linalg.solve_triangular(low_factor, panel_rows.T, lower=True).T

time: 528 us -> 511 us (0.968)
  blocking collectives: 98.4 us -> 80.5 us
    all_gather x1 -> x0, blocking collectives: 34.4 us -> none  [local(): lax.all_gather(gram_block[:, :col_block], PTS, axis=1, tiled=True)]
    all_to_all x0 -> x1, blocking collectives: none -> 21.4 us  [enter_column(): lax.all_to_all(jnp.stack(lax.axis_size(PTS) * [x_local]), axis_name=PTS,...]
where the time goes in v1:
time: 511 us; the launch traced here: 503 us
  waiting for transfers between devices  229 us (45%)
  other arithmetic  122 us (24%)
  blocking collectives  80.5 us (16%)
  local copies, waits for them, and re-layouts  25.7 us (5%)
  matrix products  23.1 us (5%)
  between operations  16.8 us (3%)
  starting transfers between devices  5.81 us (1%)
    all_gather x1, waiting for transfers between devices, local(): lax.all_gather(own_tile, PTS, axis=1, tiled=True)  155 us
    another operation x15, other arithmetic, local(): low_factor = jnp.linalg.cholesky(leading)  79.4 us
    another operation x4, other arithmetic, local(): jax.scipy.linalg.solve_triangular(low_factor, panel_rows.T, lower=True)  40.8 us
    all_gather x1, waiting for transfers between devices, gather_in_order(): blocks = lax.all_gather(blocks, axes[k], axis=0, tiled=True)  33.4 us
    all_to_all x1, waiting for transfers between devices, summed_on_arrival(): lax.all_to_all(cut_along(shard, dim, count), axis, 0, 0, tiled=True)  33.3 us
    all_gather x1, blocking collectives, local(): own_points = lax.all_gather(points, 'env', axis=1, tiled=True)  23.6 us
    all_gather x1, blocking collectives, local(): lax.all_gather(gram_block[:row_block, :], 'env', axis=0, tiled=True)  23.5 us
    all_to_all x1, blocking collectives, enter_column(): lax.all_to_all(jnp.stack(lax.axis_size(PTS) * [x_local]), axis_name=PTS,...  21.4 us
  transfers between devices with their start and end apart: 4, of which 4 were waited for; matrix products, arithmetic and copies ran while one was open for 0% of the time, Pallas kernels for 0%

profile of v1, /device:TPU:1, one launch (start us, length us, event | category | flops | bytes accessed | tf_op | source)
XLA Modules:
  0.0 503.1 jit_solution(5914022234829544233)
XLA Ops:
  7.2 12.0 %all-gather = f32[128,1024]{1,0:T(8,128)} all-gather(f32[64,1024]{1,0:T(8,128)} %param.5), channel_id=2, replica_groups=mesh['env'=16,'pts_0'=2,'pts_1'=8] {'pts_0'}, dimensions={0}, use_global_device_ids=true | all-gather | bytes 786432 | tf_op jit(solution)/shard_map/all_gather | solution.py:31
  19.3 23.6 %all_gather.20 = f32[160,1024]{0,1:T(8,128)S(1)} all-gather(f32[160,64]{0,1:T(8,128)} %param.7), channel_id=1, replica_groups=mesh['env'=16,'pts_0'=2,'pts_1'=8] {'env'}, dimensions={1}, use_global_device_ids=true | all-gather | bytes 696320 | tf_op jit(solution)/shard_map/all_gather | solution.py:76
  42.9 33.4 %all-gather.5.cloned.1.call-done = f32[16,64,1024]{2,1,0:T(8,128)} async-done(((f32[2,64,1024]{2,1,0:T(8,128)}), f32[16,64,1024]{2,1,0:T(8,128)}) %all-gather.5.cloned.1.call-update) | async-done | bytes 4194320 | tf_op jit(solution)/shard_map/all_gather | solution.py:31
  76.3 2.5 copy.33
  78.8 2.3 multiply_multiply_fusion
  81.1 154.6 %all-gather.7.cloned.1.call-done = f32[1024,2560]{0,1:T(8,128)} async-done(((f32[1024,160]{0,1:T(8,128)}), f32[1024,2560]{0,1:T(8,128)}) %all-gather.7.cloned.1.call-update) | async-done | bytes 10485776 | tf_op jit(solution)/shard_map/all_gather | solution.py:86
  235.7 10.6 %convolution_multiply_fusion = f32[2560,160]{0,1:T(8,128)} fusion(f32[1024,2560]{0,1:T(8,128)} %all-gather.7.cloned.1.call-done, f32[1024]{0:T(1024)S(1)} %copy-done.2, f32[1024,160]{0,1:T(8,128)S(1)} %get-tuple-element.57), kind=kOutput, calls=%fused_computation.2 | convolution fusion | flops 2517811200 | bytes 12783616 | tf_op jit(solution)/shard_map/dot_general | solution.py:85
  246.3 2.6 reshape_reshape_reshape.3
  248.9 3.0 copy.34
  251.9 5.7 %all-to-all-start = ((f32[16,160,160]{1,2,0:T(8,128)}), f32[16,160,160]{1,2,0:T(8,128)S(1)}, u32[]{:S(2)}, u32[]{:S(2)}) async-start(f32[16,160,160]{1,2,0:T(8,128)} %copy.34), calls=%async_computation | async-start | bytes 5242880 | tf_op jit(solution)/shard_map/all_to_all | solution.py:49
  257.6 33.3 %all-to-all-done = f32[16,160,160]{1,2,0:T(8,128)S(1)} async-done(((f32[16,160,160]{1,2,0:T(8,128)}), f32[16,160,160]{1,2,0:T(8,128)S(1)}, u32[]{:S(2)}, u32[]{:S(2)}) %all-to-all-start) | async-done | bytes 1638432 | tf_op jit(solution)/shard_map/all_to_all | solution.py:49
  291.5 21.4 %all_to_all.10 = f32[16,160,32]{1,2,0:T(8,128)S(1)} all-to-all(f32[16,160,32]{1,2,0:T(8,128)S(1)} %stack.2), channel_id=1, replica_groups=mesh['env'=16,'pts_0'=2,'pts_1'=8] {'pts_0','pts_1'}, dimensions={0} | all-to-all | bytes 655360 | tf_op jit(solution)/shard_map/all_to_all | solution.py:14
  312.9 0.7 copy.44
  313.7 0.6 iota_multiply_fusion
  314.3 23.5 %all_gather.23 = f32[512,160]{1,0:T(8,128)S(1)} all-gather(f32[32,160]{1,0:T(8,128)S(1)} %slice.148), channel_id=1, replica_groups=mesh['env'=16,'pts_0'=2,'pts_1'=8] {'env'}, dimensions={0}, use_global_device_ids=true | all-gather | bytes 348160 | tf_op jit(solution)/shard_map/all_gather | solution.py:112
  337.7 0.8 copy-done
  338.7 0.7 copy.46
  339.4 0.7 copy.45
  340.3 7.9 %all-gather.9.cloned.1.call-done = f32[512,512]{1,0:T(8,128)} async-done(((f32[32,512]{1,0:T(8,128)}), f32[512,512]{1,0:T(8,128)}) %all-gather.9.cloned.1.call-update) | async-done | bytes 1048592 | tf_op jit(solution)/shard_map/all_gather | solution.py:108
  348.2 1.6 copy.38
  349.8 1.4 fusion
  351.2 11.7 %cholesky.104 = f32[128,128]{1,0:T(8,128)S(1)} custom-call(f32[128,128]{1,0:T(8,128)S(1)} %cholesky.266), custom_call_target="Cholesky" | custom-call | tf_op jit(solution)/shard_map/jit(cholesky)/cholesky | solution.py:109
  363.1 9.8 %custom-call.30 = f32[1,128,128]{1,2,0:T(8,128)S(1)} custom-call(f32[1,128,128]{2,1,0:T(8,128)S(1)} %get-tuple-element.55), custom_call_target="InvertDiagBlocksLowerTriangular" | custom-call | tf_op jit(solution)/shard_map/jit(cholesky)/cholesky | solution.py:109
  372.9 0.3 constant_dynamic-update-slice_fusion.3
  373.2 0.3 convolution_subtract_fusion
  373.6 11.7 %cholesky.217 = f32[128,128]{1,0:T(8,128)S(1)} custom-call(f32[128,128]{1,0:T(8,128)S(1)} %cholesky.270), custom_call_target="Cholesky" | custom-call | tf_op jit(solution)/shard_map/jit(cholesky)/cholesky | solution.py:109
  385.3 9.9 %custom-call.31 = f32[1,128,128]{1,2,0:T(8,128)S(1)} custom-call(f32[1,128,128]{2,1,0:T(8,128)S(1)} %get-tuple-element.52), custom_call_target="InvertDiagBlocksLowerTriangular" | custom-call | tf_op jit(solution)/shard_map/jit(cholesky)/cholesky | solution.py:109
  395.3 0.3 convolution_dynamic-update-slice_fusion
  395.6 0.4 convolution_subtract_fusion.1
  396.0 11.7 %cholesky.238 = f32[128,128]{1,0:T(8,128)S(1)} custom-call(f32[128,128]{1,0:T(8,128)S(1)} %cholesky.275), custom_call_target="Cholesky" | custom-call | tf_op jit(solution)/shard_map/jit(cholesky)/cholesky | solution.py:109
  407.7 9.8 %custom-call.32 = f32[1,128,128]{1,2,0:T(8,128)S(1)} custom-call(f32[1,128,128]{2,1,0:T(8,128)S(1)} %get-tuple-element.49), custom_call_target="InvertDiagBlocksLowerTriangular" | custom-call | tf_op jit(solution)/shard_map/jit(cholesky)/cholesky | solution.py:109
  417.7 0.4 convolution_subtract_fusion.9
  418.1 11.9 %cholesky.255 = f32[128,128]{1,0:T(8,128)S(1)} custom-call(f32[128,128]{1,0:T(8,128)S(1)} %convolution_subtract_fusion.9), custom_call_target="Cholesky" | custom-call | tf_op jit(solution)/shard_map/jit(cholesky)/cholesky | solution.py:109
  430.0 0.6 compare_reduce_fusion.3
  430.7 0.7 compare_reduce_fusion.2
  431.4 0.6 compare_reduce_fusion.1
  432.0 0.7 compare_reduce_fusion
  435.4 0.7 triangular_solve.123
  436.0 10.9 %while.4 = (s32[]{:T(128)}, f32[512,512]{1,0:T(8,128)S(1)}, s32[4,2]{0,1:T(2,128)S(1)}, f32[4,128,128]{2,1,0:T(8,128)}, s32[]{:T(128)}) while((s32[]{:T(128)}, f32[512,512]{1,0:T(8,128)S(1)}, s32[4,2]{0,1:T(2,128)S(1)}, f32[4,128,128]{2,1,0:T(8,128)}, s32[]{:T(128)}) %tuple.46), condition=%wide.while_cond, body=%wide.while_body.sunk | while | flops 2 | bytes 132205 | solution.py:110
  436.1 0.6 fusion.71
  436.7 2.0 bitcast_dynamic-update-slice_fusion.2
  438.8 0.6 fusion.71
  439.4 2.1 bitcast_dynamic-update-slice_fusion.2
  441.5 0.6 fusion.71
  442.1 2.0 bitcast_dynamic-update-slice_fusion.2
  444.2 0.6 fusion.71
  444.8 2.1 bitcast_dynamic-update-slice_fusion.2
  446.9 40.1 %custom-call.34 = f32[4,128,128]{1,2,0:T(8,128)S(1)} custom-call(f32[4,128,128]{2,1,0:T(8,128)} %get-tuple-element.17), custom_call_target="InvertDiagBlocksLowerTriangular" | custom-call | tf_op jit(solution)/shard_map/jit(_solve_triangular)/triangular_solve | solution.py:110
  487.0 1.3 fusion.27
  488.3 0.2 fusion.33
  488.5 0.3 convolution_subtract_fusion.3
  488.8 0.2 fusion.41
  489.0 0.3 convolution_subtract_fusion.7
  489.3 0.2 fusion.43
  489.5 0.4 convolution_subtract_fusion.6
  489.9 0.2 fusion.45
  490.3 0.7 copy.43
  491.0 1.2 convolution_subtract_fusion.2
  492.2 0.2 fusion.40
  492.4 1.2 convolution_subtract_fusion.5
  493.6 0.2 fusion.42
  493.8 0.4 convolution_subtract_fusion.4
  494.2 0.2 fusion.44
  494.5 1.9 convolution_subtract_fusion.8
  (41 shorter events, 2.1 us)
Async XLA Ops:
  7.2 69.1 %all-gather.5.cloned.1.call-start = ((), (), s32[]{:S(2)}) async-start(), calls=%async_computation.2 | async-start | bytes 4718592 | tf_op jit(solution)/shard_map/all_gather | solution.py:31
  19.2 216.5 %all-gather.7.cloned.1.call-start = ((), (), s32[]{:S(2)}) async-start(), calls=%async_computation.3 | async-start | bytes 11141120 | tf_op jit(solution)/shard_map/all_gather | solution.py:86
  78.8 156.9 %copy-start.2 = (f32[1024]{0:T(1024)S(1)}, f32[1024]{0:T(1024)}, u32[]{:S(2)}) copy-start(f32[1024]{0:T(1024)} %param.6) | copy-start | bytes 12292
  251.9 39.1 %all-to-all-start = ((f32[16,160,160]{1,2,0:T(8,128)}), f32[16,160,160]{1,2,0:T(8,128)S(1)}, u32[]{:S(2)}, u32[]{:S(2)}) async-start(f32[16,160,160]{1,2,0:T(8,128)} %copy.34), calls=%async_computation | async-start | bytes 5242880 | tf_op jit(solution)/shard_map/all_to_all | solution.py:49
  257.6 90.6 %all-gather.9.cloned.1.call-start = ((), (), s32[]{:S(2)}) async-start(), calls=%async_computation.4 | async-start | bytes 1114112 | tf_op jit(solution)/shard_map/all_gather | solution.py:108
  291.3 49.0 %copy-start.1 = (f32[160,160]{1,0:T(8,128)}, f32[160,160]{1,0:T(8,128)S(1)}, u32[]{:S(2)}) copy-start(f32[160,160]{1,0:T(8,128)S(1)} %convert_add_fusion) | copy-start | bytes 307204
  337.7 0.8 copy-start
Sparse Core Ops, SparseCore 0:
  19.3 56.9 all-gather.4
  81.2 154.4 all-gather.6
  313.8 34.3 all-gather.8
